TPU v7x, 256 devices: a whole 4x4x8 slice. The times are simulated.
256 devices in a mesh: ka: 32 (over x_hi, z, core), band: 8 (over x_lo, y).
Axes of the slice: x: 4 (x_hi: 2, x_lo: 2; x = x_hi * 2 + x_lo), y: 4, z: 8, core: 2. Of those that a mesh axis runs over, the one named last changes fastest.
Arguments:
- valence_orbitals: bfloat16 [32, 32, 64, 64, 128], P('ka', None, None, 'band'), may hold values from -6 to 6
- conduction_orbitals: bfloat16 [32, 1, 64, 64, 128], P(None, None, 'ka', 'band'), may hold values from -6 to 6
- valence_energy: float32 [32, 32], P('ka'), may hold values from -1.5 to -0.1
- conduction_energy: float32 [32, 1], replicated, may hold values from 0.1 to 1.5
- valence_select: int32 [32, 16], P('ka'), may hold values from 0 to 31, as said below
- shifted_index: int32 [32], replicated, may hold values from 0 to 31, each once
- wave_vectors: int32 [3, 2048], replicated, may hold values from -16 to 15
- frequency: float32 [1], replicated, may hold values from 0.3 to 1
Outputs:
- chi_zero: float32 [2, 2048, 2048], P(None, ('ka', 'band'))
Inputs may be any that keep to these rules, and one draw needn't show every extreme that they name: `valence_select`: each row holds 16 different band numbers. `shifted_index`: every k point is the partner of exactly one k point.
All inputs are finite; a program needn't handle non-finite values.
Results may differ from a plain program's by a relative error of at most 0.025.
Values may be sent and summed in bfloat16 or wider, within the bound.
No kernel may reach another device: no remote copies, remote signals or barrier semaphores. Data moves between devices by JAX's collectives and lax.ppermute only.
A program may use at most 256 MiB of HBM per device.

v0:
```python
import math
import jax
import jax.numpy as jnp
from jax import lax
from jax.sharding import PartitionSpec as P


def depth_matrix(grid_size):
    positions = jnp.arange(grid_size, dtype=jnp.int32)
    phase_index = positions[:, None] * positions[None, :] % grid_size
    angle_value = phase_index.astype(jnp.float32) * (2.0 * math.pi / grid_size)
    cosine = jnp.cos(angle_value)
    sine_part = jnp.sin(angle_value)
    upper_half = jnp.concatenate([cosine, -sine_part], axis=1)
    lower_half = jnp.concatenate([sine_part, cosine], axis=1)
    return jnp.concatenate([upper_half, lower_half], axis=0).astype(jnp.bfloat16)


def column_matrix(grid_size):
    positions = jnp.arange(grid_size, dtype=jnp.int32)
    phase_index = positions[:, None] * positions[None, :] % grid_size
    angle_value = phase_index.astype(jnp.float32) * (2.0 * math.pi / grid_size)
    return jnp.concatenate([jnp.cos(angle_value), jnp.sin(angle_value)], axis=0).astype(
        jnp.bfloat16
    )


def shards(
    valence_orbitals,
    conduction_orbitals,
    valence_energy,
    conduction_energy,
    valence_select,
    shifted_index,
    wave_vectors,
    frequency,
):
    grid_size = valence_orbitals.shape[2]
    slab_width = valence_orbitals.shape[3]
    kpoint_count = lax.axis_size("ka")
    band_count = lax.axis_size("band")
    kpoint_rank = lax.axis_index("ka")
    band_rank = lax.axis_index("band")
    vector_count = wave_vectors.shape[1]
    block_rows = vector_count // (kpoint_count * band_count)
    share_size = vector_count // band_count
    permuted = (
        wave_vectors.reshape(3, kpoint_count, band_count, block_rows)
        .transpose(0, 2, 1, 3)
        .reshape(3, vector_count)
    )
    wrapped = jnp.mod(permuted, grid_size)
    twice = 2 * grid_size
    first_index = wrapped[1] * twice + wrapped[2]
    second_index = (grid_size + wrapped[1]) * twice + grid_size + wrapped[2]
    third_index = wrapped[1] * twice + grid_size + wrapped[2]
    fourth_index = (grid_size + wrapped[1]) * twice + wrapped[2]
    plane_coord = band_rank * slab_width + jnp.arange(slab_width, dtype=jnp.int32)
    plane_phase = wrapped[0][None, :] * plane_coord[:, None] % grid_size
    plane_angle = plane_phase.astype(jnp.float32) * (2.0 * math.pi / grid_size)
    norm_scale = float(grid_size) ** (-1.5)
    plane_cos = jnp.cos(plane_angle) * norm_scale
    plane_sin = jnp.sin(plane_angle) * norm_scale
    depth_table = depth_matrix(grid_size)
    column_table = column_matrix(grid_size)
    selected = jnp.take(valence_orbitals[0], valence_select[0], axis=0)
    selected_count = selected.shape[0]
    val_energies = jnp.take(valence_energy[0], valence_select[0])
    partner = shifted_index[kpoint_rank]
    cond_energies = lax.dynamic_index_in_dim(conduction_energy, partner, 0, keepdims=False)
    energy_gap = val_energies[None, :] - cond_energies[:, None]
    weight = (
        2.0
        * energy_gap
        / (energy_gap * energy_gap + frequency[0] * frequency[0])
        / (kpoint_count * selected_count)
    )

    def item_terms(columns):
        cond_real = columns[..., :grid_size].astype(jnp.float32)
        cond_imag = columns[..., grid_size:].astype(jnp.float32)
        val_real = selected[..., :grid_size].astype(jnp.float32)
        val_imag = selected[..., grid_size:].astype(jnp.float32)
        pair_values = jnp.concatenate(
            [
                val_real * cond_real[None] + val_imag * cond_imag[None],
                val_real * cond_imag[None] - val_imag * cond_real[None],
            ],
            axis=-1,
        ).astype(jnp.bfloat16)
        spectrum = jnp.dot(
            pair_values.reshape(-1, twice), depth_table, preferred_element_type=jnp.float32
        )
        spectrum = spectrum.astype(jnp.bfloat16).reshape(pair_values.shape)
        mixed_part = jnp.einsum(
            "ky,nyxc->nxkc", column_table, spectrum, preferred_element_type=jnp.float32
        )
        flat_view = mixed_part.reshape(selected_count, slab_width, twice * twice)
        real_cols = jnp.take(flat_view, first_index, axis=2) + jnp.take(
            flat_view, second_index, axis=2
        )
        imag_cols = jnp.take(flat_view, third_index, axis=2) - jnp.take(
            flat_view, fourth_index, axis=2
        )
        density_real = jnp.sum(plane_cos[None] * real_cols + plane_sin[None] * imag_cols, axis=1)
        density_imag = jnp.sum(plane_cos[None] * imag_cols - plane_sin[None] * real_cols, axis=1)
        return jnp.stack([density_real, density_imag])

    reordered = jnp.take(conduction_orbitals, shifted_index, axis=0)
    partial_value = lax.map(
        item_terms, lax.all_to_all(reordered, "ka", split_axis=0, concat_axis=2, tiled=True)[0]
    )
    summed = lax.psum(partial_value.astype(jnp.bfloat16), "band")
    own_share = lax.dynamic_slice_in_dim(summed, band_rank * share_size, share_size, 3)
    weighted = (weight[:, None, :, None] * own_share.astype(jnp.float32)).astype(jnp.bfloat16)
    contract_dims = (((0, 1, 2), (0, 1, 2)), ((), ()))
    swapped = jnp.stack([weighted[:, 1], -weighted[:, 0]], axis=1)
    real_rows = lax.dot_general(weighted, summed, contract_dims, preferred_element_type=jnp.float32)
    imag_rows = lax.dot_general(swapped, summed, contract_dims, preferred_element_type=jnp.float32)
    chi_block = lax.psum_scatter(
        jnp.stack([real_rows, imag_rows], axis=1).astype(jnp.bfloat16),
        "ka",
        scatter_dimension=0,
        tiled=True,
    ).astype(jnp.float32)
    chi_block = chi_block.reshape(block_rows, 2, band_count, kpoint_count, block_rows).transpose(
        0, 1, 3, 2, 4
    )
    chi_block = chi_block.reshape(block_rows, 2, vector_count)
    return chi_block.transpose(1, 0, 2)


def solution(mesh):
    in_specs = (
        P("ka", None, None, "band", None),
        P(None, None, "ka", "band", None),
        P("ka", None),
        P(),
        P("ka", None),
        P(),
        P(),
        P(),
    )
    out_specs = P(None, ("ka", "band"), None)
    return jax.shard_map(shards, mesh=mesh, in_specs=in_specs, out_specs=out_specs, check_vma=False)
```

profile of v0, /device:TPU:8, one launch (start us, length us, event | category | flops | bytes accessed | tf_op | source)
XLA Modules:
  0.0 472.1 jit_solution(15775231682070053295)
XLA Ops:
  6.5 0.0 copy-start
  6.5 0.7 compare_select_fusion.4
  7.2 0.7 compare_and_fusion.4
  7.9 0.0 copy-done
  7.9 0.6 gather_fusion.2
  8.5 0.8 bitcast_select_fusion
  9.3 11.3 %all-to-all-start = ((bf16[32,1,2,8,128]{4,3,2,1,0:T(8,128)(2,1)}), bf16[32,1,2,8,128]{4,3,2,1,0:T(8,128)(2,1)S(1)}, u32[]{:S(2)}, u32[]{:S(2)}) async-start(bf16[32,1,2,8,128]{4,3,2,1,0:T(8,128)(2,1)} %bitcast_select_fusion), calls=%async_computation | async-start | bytes 262144 | tf_op jit(solution)/shard_map/all_to_all | solution.py:111
  20.6 0.0 all-reduce.2.cloned.1.call-start
  20.6 0.7 fusion.38
  21.3 0.7 compare_and_fusion.5
  22.0 0.2 negate_convert_fusion
  22.1 1.0 reshape.231
  23.1 0.1 copy.29
  23.2 0.2 reshape.232
  23.5 0.0 copy-start.5
  23.5 4.3 gather_fusion.1
  27.9 0.0 copy-start.2
  27.9 0.0 copy-start.6
  27.9 1.9 broadcast_select_fusion
  29.8 0.3 cosine_multiply_fusion
  30.1 0.1 fusion.37
  30.3 0.0 copy-done.5
  30.3 0.6 dynamic_slice.13
  32.2 0.3 copy.30
  32.5 1.3 copy.35
  33.9 0.0 copy-done.2
  33.9 0.7 gather_fusion
  35.8 0.0 copy-done.6
  35.8 0.7 constant_dynamic-slice_fusion
  36.5 0.0 all-to-all-done
  36.5 0.1 slice_convert_fusion.1
  36.6 1.7 fusion.1
  38.3 1.3 convolution_convert_fusion
  39.7 4.6 convolution_bitcast_fusion
  44.2 49.9 %copy.44 = f32[16,8,128,128]{0,1,3,2:T(8,128)} copy(f32[16,8,128,128]{2,3,1,0:T(8,128)} %convolution_bitcast_fusion) | data formatting | bytes 16777216 | tf_op jit(solution)/shard_map/while/body/eval_jaxpr/reshape | solution.py:98
  94.1 0.0 copy-start.3
  94.1 33.5 %gather_fusion.6 = f32[2048,16,8]{1,2,0:T(8,128)} fusion(f32[16,8,16384]{0,1,2:T(8,128)} %bitcast.41, s32[2048]{0:T(1024)S(1)} %get-tuple-element.67), kind=kCustom, calls=%fused_computation.3.clone | custom fusion | bytes 2105344 | tf_op jit(solution)/shard_map/while/body/eval_jaxpr/jit(_take)/gather | solution.py:102
  127.6 33.6 %gather_fusion.3 = f32[2048,16,8]{1,2,0:T(8,128)} fusion(f32[16,8,16384]{0,1,2:T(8,128)} %bitcast.41, s32[2048]{0:T(1024)S(1)} %get-tuple-element.57), kind=kCustom, calls=%fused_computation.clone | custom fusion | bytes 2105344 | tf_op jit(solution)/shard_map/while/body/eval_jaxpr/jit(_take)/gather | solution.py:99
  161.3 33.7 %gather_fusion.5 = f32[2048,16,8]{1,2,0:T(8,128)} fusion(f32[16,8,16384]{0,1,2:T(8,128)} %bitcast.41, s32[2048]{0:T(1024)S(1)} %get-tuple-element.56), kind=kCustom, calls=%fused_computation.2.clone | custom fusion | bytes 2105344 | tf_op jit(solution)/shard_map/while/body/eval_jaxpr/jit(_take)/gather | solution.py:102
  195.0 33.5 %gather_fusion.4 = f32[2048,16,8]{1,2,0:T(8,128)} fusion(f32[16,8,16384]{0,1,2:T(8,128)} %bitcast.41, s32[2048]{0:T(1024)S(1)} %get-tuple-element.66), kind=kCustom, calls=%fused_computation.1.clone | custom fusion | bytes 2105344 | tf_op jit(solution)/shard_map/while/body/eval_jaxpr/jit(_take)/gather | solution.py:99
  228.5 0.0 copy-done.3
  228.5 0.0 copy-start.4
  228.5 21.9 %add_reduce_fusion = (bf16[16,2048]{0,1:T(8,128)(2,1)S(1)}, bf16[16,2048]{0,1:T(8,128)(2,1)S(1)}) fusion(f32[8,2048]{0,1:T(8,128)S(1)} %copy-done.3, f32[8,2048]{0,1:T(8,128)S(1)} %copy.30, f32[2048,16,8]{1,2,0:T(8,128)} %gather_fusion.4, pred[2048]{0:T(1024)(128)(4,1)S(1)} %get-tuple-element.64, f32[2048,16,8]{1,2,0:T(8,128)} %gather_fusion.3, ...), kind=kLoop, calls=%fused_computation.11 | loop fusion | flops 3604480 | bytes 4464640 | tf_op jit(solution)/shard_map/while/body/eval_jaxpr/reduce_sum | solution.py:105
  250.4 0.2 copy.39
  250.6 0.2 copy.38
  250.8 0.7 pad_maximum_fusion
  251.5 0.0 all-reduce.2.cloned.1.call-update
  251.5 0.2 reduce-scatter.4.cloned.1.call-start
  251.7 0.0 copy-done.4
  251.7 0.7 multiply_bitcast_fusion
  252.4 77.7 %all-reduce.2.cloned.1.call-done = bf16[1,2,16,2048]{3,2,1,0:T(8,128)(2,1)} async-done(((bf16[1,2,16,2048]{3,2,1,0:T(8,128)(2,1)}), bf16[1,2,16,2048]{3,2,1,0:T(8,128)(2,1)}) %all-reduce.2.cloned.1.call-update) | async-done | bytes 131088 | tf_op jit(solution)/shard_map/psum | solution.py:113
  330.1 0.8 multiply_convert_fusion
  330.9 1.4 fusion.7
  332.3 1.4 fusion.6
  333.6 0.2 maximum_bitcast_fusion
  333.8 1.5 copy.46
  335.3 0.0 reduce-scatter.4.cloned.1.call-update
  335.3 121.5 %reduce-scatter.4.cloned.1.call-done = bf16[8,4096]{1,0:T(8,128)(2,1)} async-done(((bf16[256,4096]{1,0:T(8,128)(2,1)}), bf16[8,4096]{1,0:T(8,128)(2,1)}) %reduce-scatter.4.cloned.1.call-update) | async-done | bytes 65552
  456.8 0.0 copy-start.1
  456.8 2.0 reshape.241
  458.9 3.0 copy.40
  461.8 3.4 reshape.240
  465.3 0.0 copy-done.1
  (8 shorter events, 0.1 us)
Async XLA Ops:
  6.5 1.4 copy-start
  9.3 27.2 %all-to-all-start = ((bf16[32,1,2,8,128]{4,3,2,1,0:T(8,128)(2,1)}), bf16[32,1,2,8,128]{4,3,2,1,0:T(8,128)(2,1)S(1)}, u32[]{:S(2)}, u32[]{:S(2)}) async-start(bf16[32,1,2,8,128]{4,3,2,1,0:T(8,128)(2,1)} %bitcast_select_fusion), calls=%async_computation | async-start | bytes 262144 | tf_op jit(solution)/shard_map/all_to_all | solution.py:111
  20.6 309.5 %all-reduce.2.cloned.1.call-start = ((), (), s32[]{:S(2)}) async-start(), calls=%async_computation.2 | async-start | bytes 262144 | tf_op jit(solution)/shard_map/psum | solution.py:113
  23.5 6.8 %copy-start.5 = (s32[32]{0:T(128)S(1)}, s32[32]{0:T(128)}, u32[]{:S(2)}) copy-start(s32[32]{0:T(128)} %param.15) | copy-start | bytes 388
  27.9 6.0 %copy-start.2 = (f32[1,32]{1,0:T(1,128)S(1)}, f32[1,32]{1,0:T(1,128)}, u32[]{:S(2)}) copy-start(f32[1,32]{1,0:T(1,128)} %param.12) | copy-start | bytes 388
  27.9 7.9 %copy-start.6 = (f32[32,1]{0,1:T(1,128)S(1)}, f32[32,1]{0,1:T(1,128)}, u32[]{:S(2)}) copy-start(f32[32,1]{0,1:T(1,128)} %param.13) | copy-start | bytes 388
  94.1 134.4 %copy-start.3 = (f32[8,2048]{0,1:T(8,128)S(1)}, f32[8,2048]{0,1:T(8,128)}, u32[]{:S(2)}) copy-start(f32[8,2048]{0,1:T(8,128)} %copy.35) | copy-start | bytes 196612
  228.5 23.2 %copy-start.4 = (s32[1,16]{1,0:T(1,128)S(1)}, s32[1,16]{1,0:T(1,128)}, u32[]{:S(2)}) copy-start(s32[1,16]{1,0:T(1,128)} %param.14) | copy-start | bytes 196
  251.5 205.4 %reduce-scatter.4.cloned.1.call-start = ((), (), s32[]{:S(2)}) async-start(), calls=%async_computation.3 | async-start | bytes 2162688
  456.8 8.4 %copy-start.1 = (bf16[32,1,2,8,128]{4,3,2,1,0:T(8,128)(2,1)S(1)}, bf16[32,1,2,8,128]{4,3,2,1,0:T(8,128)(2,1)}, u32[]{:S(2)}) copy-start(bf16[32,1,2,8,128]{4,3,2,1,0:T(8,128)(2,1)} %param.11) | copy-start | bytes 393220
Sparse Core Ops, SparseCore 0:
  251.6 78.4 all-reduce.1
  335.4 121.3 reduce-scatter.3
where the time goes:
time: 475 us; the launch traced here: 472 us
  local copies, waits for them, and re-layouts  204 us (43%)
  waiting for transfers between devices  199 us (42%)
  other arithmetic  32.1 us (7%)
  between operations  16.2 us (3%)
  starting transfers between devices  11.6 us (2%)
  matrix products  8.6 us (2%)
    unnamed x3, waiting for transfers between devices  122 us
    psum x1, waiting for transfers between devices, shards(): summed = lax.psum(partial_value.astype(jnp.bfloat16), 'band')  77.7 us
    reshape x1, local copies, waits for them, and re-layouts, item_terms(): flat_view = mixed_part.reshape(selected_count, slab_width, twice * twice)  49.9 us
    gather x1, local copies, waits for them, and re-layouts, item_terms(): jnp.take(flat_view, third_index, axis=2)  33.7 us
    gather x1, local copies, waits for them, and re-layouts, item_terms(): jnp.take(flat_view, first_index, axis=2)  33.6 us
    gather x1, local copies, waits for them, and re-layouts, item_terms(): jnp.take(flat_view, second_index, axis=2)  33.5 us
    gather x1, local copies, waits for them, and re-layouts, item_terms(): jnp.take(flat_view, fourth_index, axis=2)  33.5 us
    reduce_sum x1, other arithmetic, item_terms(): jnp.sum(plane_cos[None] * real_cols + plane_sin[None] * imag_cols, axis=1)  21.9 us
  transfers between devices with their start and end apart: 3, of which 2 were waited for; matrix products, arithmetic and copies ran while one was open for 3% of the time, Pallas kernels for 0%

commit v1 on v0

--- a/solution.py
+++ b/solution.py
@@ -110,7 +110,9 @@
     partial_value = lax.map(
         item_terms, lax.all_to_all(reordered, "ka", split_axis=0, concat_axis=2, tiled=True)[0]
     )
-    summed = lax.psum(partial_value.astype(jnp.bfloat16), "band")
+    x = partial_value.astype(jnp.bfloat16)
+    pieces = lax.all_gather(x, "band", axis=0, tiled=False)
+    summed = pieces.sum(axis=0)
     own_share = lax.dynamic_slice_in_dim(summed, band_rank * share_size, share_size, 3)
     weighted = (weight[:, None, :, None] * own_share.astype(jnp.float32)).astype(jnp.bfloat16)
     contract_dims = (((0, 1, 2), (0, 1, 2)), ((), ()))

time: 475 us -> 432 us (0.909)
  waiting for transfers between devices: 199 us -> 157 us
    psum x1 -> x0, waiting for transfers between devices: 77.7 us -> none  [shards(): summed = lax.psum(partial_value.astype(jnp.bfloat16), 'band')]
    all_gather x0 -> x1, waiting for transfers between devices: none -> 34.9 us  [shards(): pieces = lax.all_gather(x, 'band', axis=0, tiled=False)]
  transfers between devices with their start and end apart: 3 -> 3, of which waited for: 2 -> 3; matrix products, arithmetic and copies ran while one was open for 3% -> 3% of each run, Pallas kernels for 0% -> 0%
where the time goes in v1:
time: 432 us; the launch traced here: 428 us
  local copies, waits for them, and re-layouts  204 us (47%)
  waiting for transfers between devices  157 us (36%)
  other arithmetic  32.6 us (8%)
  between operations  16 us (4%)
  starting transfers between devices  11.6 us (3%)
  matrix products  6.85 us (2%)
    unnamed x3, waiting for transfers between devices  121 us
    reshape x1, local copies, waits for them, and re-layouts, item_terms(): flat_view = mixed_part.reshape(selected_count, slab_width, twice * twice)  49.9 us
    all_gather x1, waiting for transfers between devices, shards(): pieces = lax.all_gather(x, 'band', axis=0, tiled=False)  34.9 us
    gather x1, local copies, waits for them, and re-layouts, item_terms(): jnp.take(flat_view, third_index, axis=2)  33.7 us
    gather x1, local copies, waits for them, and re-layouts, item_terms(): jnp.take(flat_view, first_index, axis=2)  33.6 us
    gather x1, local copies, waits for them, and re-layouts, item_terms(): jnp.take(flat_view, second_index, axis=2)  33.5 us
    gather x1, local copies, waits for them, and re-layouts, item_terms(): jnp.take(flat_view, fourth_index, axis=2)  33.5 us
    reduce_sum x1, other arithmetic, item_terms(): jnp.sum(plane_cos[None] * real_cols + plane_sin[None] * imag_cols, axis=1)  21.9 us
  transfers between devices with their start and end apart: 3, of which 3 were waited for; matrix products, arithmetic and copies ran while one was open for 3% of the time, Pallas kernels for 0%

profile of v1, /device:TPU:8, one launch (start us, length us, event | category | flops | bytes accessed | tf_op | source)
XLA Modules:
  0.0 428.3 jit_solution(132215848327088559)
XLA Ops:
  6.5 0.0 copy-start
  6.5 0.7 compare_select_fusion.4
  7.2 0.7 compare_and_fusion.4
  7.9 0.0 copy-done
  7.9 0.6 gather_fusion.2
  8.5 0.8 bitcast_select_fusion
  9.3 11.3 %all-to-all-start = ((bf16[32,1,2,8,128]{4,3,2,1,0:T(8,128)(2,1)}), bf16[32,1,2,8,128]{4,3,2,1,0:T(8,128)(2,1)S(1)}, u32[]{:S(2)}, u32[]{:S(2)}) async-start(bf16[32,1,2,8,128]{4,3,2,1,0:T(8,128)(2,1)} %bitcast_select_fusion), calls=%async_computation | async-start | bytes 262144 | tf_op jit(solution)/shard_map/all_to_all | solution.py:111
  20.6 0.0 all-gather.2.cloned.1.call-start
  20.6 0.7 fusion.36
  21.3 0.7 compare_and_fusion.5
  22.0 0.2 negate_convert_fusion
  22.1 1.0 reshape.239
  23.1 0.1 copy.38
  23.2 0.2 reshape.240
  23.5 4.3 %gather_fusion.1 = bf16[16,64,8,128]{3,2,1,0:T(8,128)(2,1)} fusion(bf16[32,64,8,128]{3,2,1,0:T(8,128)(2,1)} %bitcast.116, s32[1024]{0:T(1024)S(1)} %pad_clamp_fusion.1), kind=kCustom, calls=%fused_computation.5 | custom fusion | bytes 4194368 | tf_op jit(solution)/shard_map/jit(_take)/gather | solution.py:66
  27.9 1.8 broadcast_select_fusion
  29.7 0.3 cosine_multiply_fusion
  30.1 0.1 fusion.34
  30.2 0.3 copy.39
  30.6 1.3 copy.44
  31.9 0.6 all-to-all-done
  32.5 0.1 slice_convert_fusion.1
  32.6 1.7 fusion.1
  34.4 1.3 convolution_convert_fusion
  35.7 4.6 %convolution_bitcast_fusion = f32[16,8,128,128]{2,3,1,0:T(8,128)} fusion(bf16[16,64,8,128]{3,2,1,0:T(8,128)(2,1)S(1)} %bitcast.109, bf16[64,64]{0,1:T(8,128)(2,1)S(1)} %fusion.34, bf16[64,64]{0,1:T(8,128)(2,1)S(1)} %get-tuple-element.69), kind=kOutput, calls=%fused_computation.20 | convolution fusion | flops 268468224 | bytes 10502144 | tf_op jit(solution)/shard_map/while/body/eval_jaxpr/ky,nyxc->nxkc/dot_general | solution.py:95
  40.3 49.9 %copy.53 = f32[16,8,128,128]{0,1,3,2:T(8,128)} copy(f32[16,8,128,128]{2,3,1,0:T(8,128)} %convolution_bitcast_fusion) | data formatting | bytes 16777216 | tf_op jit(solution)/shard_map/while/body/eval_jaxpr/reshape | solution.py:98
  90.1 0.0 copy-start.3
  90.1 33.5 %gather_fusion.6 = f32[2048,16,8]{1,2,0:T(8,128)} fusion(f32[16,8,16384]{0,1,2:T(8,128)} %bitcast.40, s32[2048]{0:T(1024)S(1)} %get-tuple-element.67), kind=kCustom, calls=%fused_computation.3.clone | custom fusion | bytes 2105344 | tf_op jit(solution)/shard_map/while/body/eval_jaxpr/jit(_take)/gather | solution.py:102
  123.7 33.6 %gather_fusion.3 = f32[2048,16,8]{1,2,0:T(8,128)} fusion(f32[16,8,16384]{0,1,2:T(8,128)} %bitcast.40, s32[2048]{0:T(1024)S(1)} %get-tuple-element.57), kind=kCustom, calls=%fused_computation.clone | custom fusion | bytes 2105344 | tf_op jit(solution)/shard_map/while/body/eval_jaxpr/jit(_take)/gather | solution.py:99
  157.3 33.7 %gather_fusion.5 = f32[2048,16,8]{1,2,0:T(8,128)} fusion(f32[16,8,16384]{0,1,2:T(8,128)} %bitcast.40, s32[2048]{0:T(1024)S(1)} %get-tuple-element.56), kind=kCustom, calls=%fused_computation.2.clone | custom fusion | bytes 2105344 | tf_op jit(solution)/shard_map/while/body/eval_jaxpr/jit(_take)/gather | solution.py:102
  191.0 33.5 %gather_fusion.4 = f32[2048,16,8]{1,2,0:T(8,128)} fusion(f32[16,8,16384]{0,1,2:T(8,128)} %bitcast.40, s32[2048]{0:T(1024)S(1)} %get-tuple-element.66), kind=kCustom, calls=%fused_computation.1.clone | custom fusion | bytes 2105344 | tf_op jit(solution)/shard_map/while/body/eval_jaxpr/jit(_take)/gather | solution.py:99
  224.5 0.0 copy-done.3
  224.5 0.0 copy-start.5
  224.5 0.0 copy-start.2
  224.5 0.0 copy-start.6
  224.6 0.0 copy-start.4
  224.6 21.9 %add_reduce_fusion = (bf16[16,2048]{0,1:T(8,128)(2,1)S(1)}, bf16[16,2048]{0,1:T(8,128)(2,1)S(1)}) fusion(f32[8,2048]{0,1:T(8,128)S(1)} %copy-done.3, f32[8,2048]{0,1:T(8,128)S(1)} %copy.39, f32[2048,16,8]{1,2,0:T(8,128)} %gather_fusion.4, pred[2048]{0:T(1024)(128)(4,1)S(1)} %get-tuple-element.64, f32[2048,16,8]{1,2,0:T(8,128)} %gather_fusion.3, ...), kind=kLoop, calls=%fused_computation.11 | loop fusion | flops 3604480 | bytes 4464640 | tf_op jit(solution)/shard_map/while/body/eval_jaxpr/reduce_sum | solution.py:105
  246.4 0.2 copy.47
  246.6 0.2 copy.48
  246.8 0.7 pad_maximum_fusion
  247.5 0.0 all-gather.2.cloned.1.call-update
  247.5 0.2 reduce-scatter.4.cloned.1.call-start
  247.7 0.0 copy-done.5
  247.7 0.6 dynamic_slice.11
  249.5 0.0 copy-done.2
  249.5 0.7 gather_fusion
  251.4 0.0 copy-done.6
  251.4 0.6 constant_dynamic-slice_fusion
  252.0 0.0 copy-done.4
  252.0 0.6 multiply_bitcast_fusion
  252.5 34.9 %all-gather.2.cloned.1.call-done = bf16[8,1,2,16,2048]{4,3,2,1,0:T(8,128)(2,1)} async-done(((bf16[1,1,2,16,2048]{4,3,2,1,0:T(8,128)(2,1)}), bf16[8,1,2,16,2048]{4,3,2,1,0:T(8,128)(2,1)}) %all-gather.2.cloned.1.call-update) | async-done | bytes 1048592 | tf_op jit(solution)/shard_map/all_gather | solution.py:114
  287.5 1.4 reduce_sum.34
  288.9 0.1 fusion.35
  288.9 0.5 fusion.7
  289.5 0.4 fusion.6
  289.9 0.2 maximum_bitcast_fusion
  290.1 1.5 copy.55
  291.6 0.0 reduce-scatter.4.cloned.1.call-update
  291.6 121.4 %reduce-scatter.4.cloned.1.call-done = bf16[8,4096]{1,0:T(8,128)(2,1)} async-done(((bf16[256,4096]{1,0:T(8,128)(2,1)}), bf16[8,4096]{1,0:T(8,128)(2,1)}) %reduce-scatter.4.cloned.1.call-update) | async-done | bytes 65552
  413.0 0.0 copy-start.1
  413.0 2.0 reshape.247
  415.0 3.0 copy.49
  418.0 3.4 reshape.246
  421.4 0.0 copy-done.1
  (8 shorter events, 0.1 us)
Async XLA Ops:
  6.5 1.4 copy-start
  9.3 23.3 %all-to-all-start = ((bf16[32,1,2,8,128]{4,3,2,1,0:T(8,128)(2,1)}), bf16[32,1,2,8,128]{4,3,2,1,0:T(8,128)(2,1)S(1)}, u32[]{:S(2)}, u32[]{:S(2)}) async-start(bf16[32,1,2,8,128]{4,3,2,1,0:T(8,128)(2,1)} %bitcast_select_fusion), calls=%async_computation | async-start | bytes 262144 | tf_op jit(solution)/shard_map/all_to_all | solution.py:111
  20.6 266.9 %all-gather.2.cloned.1.call-start = ((), (), s32[]{:S(2)}) async-start(), calls=%async_computation.2 | async-start | bytes 1179648 | tf_op jit(solution)/shard_map/all_gather | solution.py:114
  90.1 134.4 %copy-start.3 = (f32[8,2048]{0,1:T(8,128)S(1)}, f32[8,2048]{0,1:T(8,128)}, u32[]{:S(2)}) copy-start(f32[8,2048]{0,1:T(8,128)} %copy.44) | copy-start | bytes 196612
  224.5 23.2 %copy-start.5 = (s32[32]{0:T(128)S(1)}, s32[32]{0:T(128)}, u32[]{:S(2)}) copy-start(s32[32]{0:T(128)} %param.15) | copy-start | bytes 388
  224.5 24.9 %copy-start.2 = (f32[1,32]{1,0:T(1,128)S(1)}, f32[1,32]{1,0:T(1,128)}, u32[]{:S(2)}) copy-start(f32[1,32]{1,0:T(1,128)} %param.12) | copy-start | bytes 388
  224.5 26.8 %copy-start.6 = (f32[32,1]{0,1:T(1,128)S(1)}, f32[32,1]{0,1:T(1,128)}, u32[]{:S(2)}) copy-start(f32[32,1]{0,1:T(1,128)} %param.13) | copy-start | bytes 388
  224.6 27.4 %copy-start.4 = (s32[1,16]{1,0:T(1,128)S(1)}, s32[1,16]{1,0:T(1,128)}, u32[]{:S(2)}) copy-start(s32[1,16]{1,0:T(1,128)} %param.14) | copy-start | bytes 196
  247.5 165.5 %reduce-scatter.4.cloned.1.call-start = ((), (), s32[]{:S(2)}) async-start(), calls=%async_computation.3 | async-start | bytes 2162688
  413.0 8.4 %copy-start.1 = (bf16[32,1,2,8,128]{4,3,2,1,0:T(8,128)(2,1)S(1)}, bf16[32,1,2,8,128]{4,3,2,1,0:T(8,128)(2,1)}, u32[]{:S(2)}) copy-start(bf16[32,1,2,8,128]{4,3,2,1,0:T(8,128)(2,1)} %param.11) | copy-start | bytes 393220
Sparse Core Ops, SparseCore 0:
  247.6 39.8 all-gather.1
  291.7 121.2 reduce-scatter.3
